TPU v7x, 32 devices: a whole 2x2x4 slice. The times are simulated.
32 devices in a mesh: strip: 8 (over y, x, core), mode: 4 (over z).
Axes of the slice: x: 2, y: 2, z: 4, core: 2. Of those that a mesh axis runs over, the one named last changes fastest.
Arguments:
- object_field: float32 [2, 2048, 384], P(None, 'strip'), may hold values from -5 to 5
- probe_modes: float32 [2, 8, 256, 256], P(None, 'mode'), may hold values from -2.5 to 2.5
- measured: float32 [8, 4, 256, 256], P('strip'), may hold values from 0.1 to 27
- positions: int32 [8, 4, 2], P('strip'), may hold values from 0 to 128, as said below
Outputs:
- object_new: float32 [2, 2048, 384], P(None, 'strip')
Inputs may be any that keep to these rules, and one draw needn't show every extreme that they name: positions[s,k,0] is the first row of window k within strip s and positions[s,k,1] its first column; the windows of every strip form a two by two raster with small offsets: windows 0 and 3 start at row 128, windows 1 and 2 at row 0, window 1 at column 128, window 3 at most 16 columns left of it, windows 0 and 2 at columns 0 to 16.
All inputs are finite; a program needn't handle non-finite values.
Results may differ from a plain program's by a relative error of at most 0.0001.
Values sent between devices are 32-bit elements; how exact they have to be, the bound alone decides.
A program may use at most 128 MiB of HBM per device.

v0:
```python
import jax
import jax.numpy as jnp
from jax import lax
from jax.sharding import PartitionSpec as P

HALO = 128
ITERS = 3
regularizer = 0.1
step_scale = 0.3
epsilon = 1e-06
highest = lax.Precision.HIGHEST


def from_behind(block, axis, distance):
    devices = range(lax.axis_size(axis))
    route = [(i - distance, i) for i in devices if i - distance in devices]
    return lax.ppermute(block, axis, route)


def dft_tables(length):
    indices = jnp.arange(length, dtype=jnp.int32)
    phases = indices[:, None] * indices[None, :] % length
    angles = phases.astype(jnp.float32) * (2.0 * jnp.pi / length)
    scaling = 1.0 / jnp.sqrt(jnp.float32(length))
    return (jnp.cos(angles) * scaling, -jnp.sin(angles) * scaling)


def transform(part_real, part_imag, cosine_table, sine_table):
    length = cosine_table.shape[0]
    stacked_rows = jnp.concatenate([cosine_table, sine_table], axis=0)
    left_real = jnp.einsum("jk,bkl->bjl", stacked_rows, part_real, precision=highest)
    left_imag = jnp.einsum("jk,bkl->bjl", stacked_rows, part_imag, precision=highest)
    middle_real = left_real[:, :length] - left_imag[:, length:]
    middle_imag = left_imag[:, :length] + left_real[:, length:]
    stacked_cols = jnp.concatenate([cosine_table, sine_table], axis=1)
    right_real = jnp.einsum("bjk,kl->bjl", middle_real, stacked_cols, precision=highest)
    right_imag = jnp.einsum("bjk,kl->bjl", middle_imag, stacked_cols, precision=highest)
    return (
        right_real[..., :length] - right_imag[..., length:],
        right_imag[..., :length] + right_real[..., length:],
    )


def body(object_field, probe_modes, measured, positions):
    stripe_rows = object_field.shape[1]
    width_cols = object_field.shape[2]
    window = probe_modes.shape[2]
    local_modes = probe_modes.shape[1]
    slots = positions.shape[1]
    halo_rows = HALO
    cosine_table, sine_table = dft_tables(window)
    rows_at = positions[0, :, 0]
    cols_at = positions[0, :, 1]
    total_cells = stripe_rows * lax.axis_size("strip") * width_cols
    measured_intensity = measured[0]
    probe_real = probe_modes[0][None]
    probe_imag = probe_modes[1][None]
    zero_index = jnp.zeros((), jnp.int32)
    for iteration in range(ITERS):
        below = from_behind(object_field[:, :halo_rows], "strip", -1)
        frame = jnp.concatenate([object_field, below], axis=1)
        patches = jnp.stack(
            [
                lax.dynamic_slice(
                    frame, (zero_index, rows_at[slot], cols_at[slot]), (2, window, window)
                )
                for slot in range(slots)
            ],
            axis=1,
        )
        patch_real = patches[0][:, None]
        patch_imag = patches[1][:, None]
        exit_real = probe_real * patch_real - probe_imag * patch_imag
        exit_imag = probe_real * patch_imag + probe_imag * patch_real
        far_real, far_imag = transform(
            exit_real.reshape(-1, window, window),
            exit_imag.reshape(-1, window, window),
            cosine_table,
            sine_table,
        )
        far_real = far_real.reshape(slots, local_modes, window, window)
        far_imag = far_imag.reshape(slots, local_modes, window, window)
        probe_power = jnp.sum(far_real * far_real + far_imag * far_imag, axis=1)
        summed_power = lax.psum(probe_power, "mode")
        object_update = (
            jnp.sqrt((measured_intensity + regularizer) / (summed_power + regularizer)) - 1.0
        )
        shift_real = (object_update[:, None] * far_real).reshape(-1, window, window)
        shift_imag = (object_update[:, None] * far_imag).reshape(-1, window, window)
        delta_real, delta_imag = transform(shift_real, shift_imag, cosine_table, -sine_table)
        delta_real = delta_real.reshape(slots, local_modes, window, window)
        delta_imag = delta_imag.reshape(slots, local_modes, window, window)
        grad_real = jnp.sum(probe_real * delta_real + probe_imag * delta_imag, axis=1)
        grad_imag = jnp.sum(probe_real * delta_imag - probe_imag * delta_real, axis=1)
        grad_real, grad_imag = lax.psum((grad_real, grad_imag), "mode")
        frame_grad = jnp.zeros((2, stripe_rows + halo_rows, width_cols), jnp.float32)
        for slot in range(slots):
            start = (zero_index, rows_at[slot], cols_at[slot])
            current = lax.dynamic_slice(frame_grad, start, (2, window, window))
            frame_grad = lax.dynamic_update_slice(
                frame_grad, current + jnp.stack([grad_real[slot], grad_imag[slot]]), start
            )
        arrived = from_behind(frame_grad[:, stripe_rows:], "strip", 1)
        gradient = jnp.concatenate(
            [frame_grad[:, :halo_rows] + arrived, frame_grad[:, halo_rows:stripe_rows]], axis=1
        )
        square_sum = lax.psum(jnp.sum(gradient * gradient), "strip")
        step_factor = step_scale / jnp.sqrt(square_sum / total_cells + epsilon)
        object_field = object_field + step_factor * gradient
    return object_field


def solution(mesh):
    return jax.shard_map(
        body,
        mesh=mesh,
        in_specs=(
            P(None, "strip", None),
            P(None, "mode", None, None),
            P("strip", None, None, None),
            P("strip", None, None),
        ),
        out_specs=P(None, "strip", None),
        check_vma=False,
    )
```

profile of v0, /device:TPU:4, one launch (start us, length us, event | category | flops | bytes accessed | tf_op | source)
XLA Modules:
  0.0 812.3 jit_solution(13496103538297187486)
XLA Ops:
  31.6 7.1 convolution_bitcast_fusion.10
  38.7 7.5 convolution_bitcast_fusion.11
  58.5 51.5 %all-reduce.10.cloned.1.call-done = f32[4,256,256]{2,1,0:T(8,128)} async-done(((f32[4,256,256]{2,1,0:T(8,128)}), f32[4,256,256]{2,1,0:T(8,128)}) %all-reduce.10.cloned.1.call-update) | async-done | bytes 1048592 | tf_op jit(solution)/shard_map/psum | solution.py:84
  115.7 7.2 convolution_bitcast_fusion.9
  122.9 7.6 convolution_bitcast_fusion.8
  140.1 85.5 %all-reduce.20.cloned.1.call-done = (f32[4,256,256]{2,1,0:T(8,128)}, f32[4,256,256]{2,1,0:T(8,128)}) async-done(((f32[4,256,256]{2,1,0:T(8,128)}, f32[4,256,256]{2,1,0:T(8,128)}), (f32[4,256,256]{2,1,0:T(8,128)}, f32[4,256,256]{2,1,0:T(8,128)})) %all-reduce.20.cloned.1.call-update) | async-done | bytes 2097168 | tf_op jit(solution)/shard_map/psum | solution.py:95
  228.8 6.6 dynamic_update_slice.36
  243.2 8.1 dynamic_update_slice.38
  252.5 6.6 dynamic_update_slice.39
  261.1 8.1 collective-permute-done.1
  270.8 12.5 %psum.87 = f32[]{:T(128)} all-reduce(f32[]{:T(128)} %multiply_reduce_fusion.2), channel_id=1, replica_groups=mesh['strip'=8,'mode'=4] {'strip'}, use_global_device_ids=true, to_apply=%region_7.8 | all-reduce | flops 1 | bytes 8 | tf_op jit(solution)/shard_map/psum | solution.py:107
  294.6 7.1 convolution_bitcast_fusion.6
  301.7 7.3 convolution_bitcast_fusion.7
  320.6 51.1 %all-reduce.12.cloned.1.call-done = f32[4,256,256]{2,1,0:T(8,128)} async-done(((f32[4,256,256]{2,1,0:T(8,128)}), f32[4,256,256]{2,1,0:T(8,128)}) %all-reduce.12.cloned.1.call-update) | async-done | bytes 1048592 | tf_op jit(solution)/shard_map/psum | solution.py:84
  377.4 7.2 convolution_bitcast_fusion.5
  384.6 7.4 convolution_bitcast_fusion.4
  401.5 85.5 %all-reduce.18.cloned.1.call-done = (f32[4,256,256]{2,1,0:T(8,128)}, f32[4,256,256]{2,1,0:T(8,128)}) async-done(((f32[4,256,256]{2,1,0:T(8,128)}, f32[4,256,256]{2,1,0:T(8,128)}), (f32[4,256,256]{2,1,0:T(8,128)}, f32[4,256,256]{2,1,0:T(8,128)})) %all-reduce.18.cloned.1.call-update) | async-done | bytes 2097168 | tf_op jit(solution)/shard_map/psum | solution.py:95
  490.2 6.6 dynamic_update_slice.40
  504.6 8.1 dynamic_update_slice.42
  513.9 6.6 dynamic_update_slice.43
  522.5 8.1 collective-permute-done.3
  532.2 12.5 %psum.91 = f32[]{:T(128)} all-reduce(f32[]{:T(128)} %multiply_reduce_fusion.1), channel_id=1, replica_groups=mesh['strip'=8,'mode'=4] {'strip'}, use_global_device_ids=true, to_apply=%region_15.16 | all-reduce | flops 1 | bytes 8 | tf_op jit(solution)/shard_map/psum | solution.py:107
  556.1 7.1 convolution_bitcast_fusion.2
  563.1 7.2 convolution_bitcast_fusion.3
  581.7 51.3 %all-reduce.14.cloned.1.call-done = f32[4,256,256]{2,1,0:T(8,128)} async-done(((f32[4,256,256]{2,1,0:T(8,128)}), f32[4,256,256]{2,1,0:T(8,128)}) %all-reduce.14.cloned.1.call-update) | async-done | bytes 1048592 | tf_op jit(solution)/shard_map/psum | solution.py:84
  639.0 7.2 convolution_bitcast_fusion.1
  646.2 7.6 convolution_bitcast_fusion
  663.3 85.6 %all-reduce.16.cloned.1.call-done = (f32[4,256,256]{2,1,0:T(8,128)}, f32[4,256,256]{2,1,0:T(8,128)}) async-done(((f32[4,256,256]{2,1,0:T(8,128)}, f32[4,256,256]{2,1,0:T(8,128)}), (f32[4,256,256]{2,1,0:T(8,128)}, f32[4,256,256]{2,1,0:T(8,128)})) %all-reduce.16.cloned.1.call-update) | async-done | bytes 2097168 | tf_op jit(solution)/shard_map/psum | solution.py:95
  751.9 6.8 dynamic_update_slice.44
  765.4 8.1 dynamic_update_slice.46
  782.2 8.1 collective-permute-done.5
  791.2 12.5 %psum.95 = f32[]{:T(128)} all-reduce(f32[]{:T(128)} %multiply_reduce_fusion), channel_id=1, replica_groups=mesh['strip'=8,'mode'=4] {'strip'}, use_global_device_ids=true, to_apply=%region_23.24 | all-reduce | flops 1 | bytes 8 | tf_op jit(solution)/shard_map/psum | solution.py:107
  (133 shorter events, 163.9 us)
Async XLA Ops:
  6.5 23.4 %copy-start.11 = (f32[2,2,256,256]{3,2,1,0:T(8,128)S(1)}, f32[2,2,256,256]{3,2,1,0:T(8,128)}, u32[]{:S(2)}) copy-start(f32[2,2,256,256]{3,2,1,0:T(8,128)} %param.5) | copy-start | bytes 3145732
  6.5 103.5 %all-reduce.10.cloned.1.call-start = ((), (), s32[]{:S(2)}) async-start(), calls=%async_computation | async-start | bytes 2097152 | tf_op jit(solution)/shard_map/psum | solution.py:84
  8.4 21.7 %collective-permute-start = (f32[2,128,384]{2,1,0:T(8,128)}, f32[2,128,384]{2,1,0:T(8,128)S(1)}, u32[]{:S(2)}, u32[]{:S(2)}) collective-permute-start(f32[2,128,384]{2,1,0:T(8,128)} %slice.359), channel_id=1, source_target_pairs={{4,0},{8,4},{12,8},{16,12},{20,16},{24,20},{28,24},{5,1},{9,5},{13... | collective-permute-start | bytes 1179656 | tf_op jit(solution)/shard_map/ppermute | solution.py:17
  50.0 3.7 copy-start
  53.7 1.9 copy-start.1
  55.7 54.3 %copy-start.7 = (f32[1,4,256,256]{3,2,1,0:T(8,128)S(1)}, f32[1,4,256,256]{3,2,1,0:T(8,128)}, u32[]{:S(2)}) copy-start(f32[1,4,256,256]{3,2,1,0:T(8,128)} %param.6) | copy-start | bytes 3145732
  57.4 168.2 %all-reduce.20.cloned.1.call-start = ((), (), s32[]{:S(2)}) async-start(), calls=%async_computation.5 | async-start | bytes 4194304 | tf_op jit(solution)/shard_map/psum | solution.py:95
  140.0 231.6 %all-reduce.12.cloned.1.call-start = ((), (), s32[]{:S(2)}) async-start(), calls=%async_computation.1 | async-start | bytes 2097152 | tf_op jit(solution)/shard_map/psum | solution.py:84
  225.6 2.2 copy-start.12
  259.1 10.0 %collective-permute-start.1 = (f32[2,128,384]{2,1,0:T(8,128)S(1)}, f32[2,128,384]{2,1,0:T(8,128)S(1)}, u32[]{:S(2)}, u32[]{:S(2)}) collective-permute-start(f32[2,128,384]{2,1,0:T(8,128)S(1)} %slice.485), channel_id=1, source_target_pairs={{0,4},{4,8},{8,12},{12,16},{16,20},{20,24},{24,28},{1,5},{5,9},{9,... | collective-permute-start | bytes 1179656 | tf_op jit(solution)/shard_map/ppermute | solution.py:17
  269.2 0.7 copy-start.10
  285.3 8.6 %copy-start.6 = (f32[2,256,384]{2,1,0:T(8,128)}, f32[2,256,384]{2,1,0:T(8,128)S(1)}, u32[]{:S(2)}) copy-start(f32[2,256,384]{2,1,0:T(8,128)S(1)} %multiply_add_fusion.8) | copy-start | bytes 2359300
  285.3 7.2 collective-permute-start.2
  312.7 3.7 copy-start.4
  316.5 1.9 copy-start.5
  318.4 53.2 %copy-start.8 = (f32[1,4,256,256]{3,2,1,0:T(8,128)S(1)}, f32[1,4,256,256]{3,2,1,0:T(8,128)}, u32[]{:S(2)}) copy-start(f32[1,4,256,256]{3,2,1,0:T(8,128)} %param.6) | copy-start | bytes 3145732
  320.0 167.0 %all-reduce.18.cloned.1.call-start = ((), (), s32[]{:S(2)}) async-start(), calls=%async_computation.4 | async-start | bytes 4194304 | tf_op jit(solution)/shard_map/psum | solution.py:95
  401.4 231.6 %all-reduce.14.cloned.1.call-start = ((), (), s32[]{:S(2)}) async-start(), calls=%async_computation.2 | async-start | bytes 2097152 | tf_op jit(solution)/shard_map/psum | solution.py:84
  487.0 2.2 copy-start.13
  520.5 10.0 %collective-permute-start.3 = (f32[2,128,384]{2,1,0:T(8,128)S(1)}, f32[2,128,384]{2,1,0:T(8,128)S(1)}, u32[]{:S(2)}, u32[]{:S(2)}) collective-permute-start(f32[2,128,384]{2,1,0:T(8,128)S(1)} %slice.515), channel_id=1, source_target_pairs={{0,4},{4,8},{8,12},{12,16},{16,20},{20,24},{24,28},{1,5},{5,9},{9,... | collective-permute-start | bytes 1179656 | tf_op jit(solution)/shard_map/ppermute | solution.py:17
  530.6 0.7 copy-start.9
  546.8 7.2 collective-permute-start.4
  574.1 3.7 copy-start.2
  577.8 1.9 copy-start.3
  581.4 167.5 %all-reduce.16.cloned.1.call-start = ((), (), s32[]{:S(2)}) async-start(), calls=%async_computation.3 | async-start | bytes 4194304 | tf_op jit(solution)/shard_map/psum | solution.py:95
  748.9 2.1 copy-start.14
  780.3 10.0 %collective-permute-start.5 = (f32[2,128,384]{2,1,0:T(8,128)S(1)}, f32[2,128,384]{2,1,0:T(8,128)S(1)}, u32[]{:S(2)}, u32[]{:S(2)}) collective-permute-start(f32[2,128,384]{2,1,0:T(8,128)S(1)} %slice.545), channel_id=1, source_target_pairs={{0,4},{4,8},{8,12},{12,16},{16,20},{20,24},{24,28},{1,5},{5,9},{9,... | collective-permute-start | bytes 1179656 | tf_op jit(solution)/shard_map/ppermute | solution.py:17
Sparse Core Ops, SparseCore 0:
  57.6 52.3 all-reduce.9
  140.1 85.4 all-reduce.19
  320.2 51.4 all-reduce.11
  401.5 85.4 all-reduce.17
  581.5 51.4 all-reduce.13
  663.4 85.4 all-reduce.15
where the time goes:
time: 822 us; the launch traced here: 812 us
  waiting for transfers between devices  445 us (54%)
  matrix products  132 us (16%)
  local copies, waits for them, and re-layouts  102 us (12%)
  other arithmetic  50.7 us (6%)
  blocking collectives  37.5 us (5%)
  between operations  31.3 us (4%)
  starting transfers between devices  13.8 us (2%)
    psum x3, waiting for transfers between devices, body(): grad_real, grad_imag = lax.psum((grad_real, grad_imag), 'mode')  257 us
    psum x3, waiting for transfers between devices, body(): summed_power = lax.psum(probe_power, 'mode')  154 us
    dynamic_update_slice x12, local copies, waits for them, and re-layouts, body(): lax.dynamic_update_slice(frame_grad, current + jnp.stack([grad_real[slot]...  79.7 us
    dot_general x6, matrix products, transform(): jnp.einsum('jk,bkl->bjl', stacked_rows, part_imag, precision=highest)  43.8 us
    dot_general x6, matrix products, transform(): jnp.einsum('jk,bkl->bjl', stacked_rows, part_real, precision=highest)  43.7 us
    psum x3, blocking collectives, body(): square_sum = lax.psum(jnp.sum(gradient * gradient), 'strip')  37.5 us
    ppermute x6, waiting for transfers between devices, from_behind(): return lax.ppermute(block, axis, route)  34.2 us
    dot_general x6, matrix products, transform(): jnp.einsum('bjk,kl->bjl', middle_real, stacked_cols, precision=highest)  22.2 us
  transfers between devices with their start and end apart: 12, of which 11 were waited for; matrix products, arithmetic and copies ran while one was open for 1% of the time, Pallas kernels for 0%

commit v1 on v0

--- a/solution.py
+++ b/solution.py
@@ -81,7 +81,7 @@
         far_real = far_real.reshape(slots, local_modes, window, window)
         far_imag = far_imag.reshape(slots, local_modes, window, window)
         probe_power = jnp.sum(far_real * far_real + far_imag * far_imag, axis=1)
-        summed_power = lax.psum(probe_power, "mode")
+        summed_power = jnp.sum(lax.all_gather(probe_power, "mode"), axis=0)
         object_update = (
             jnp.sqrt((measured_intensity + regularizer) / (summed_power + regularizer)) - 1.0
         )

time: 822 us -> 918 us (1.12)
  waiting for transfers between devices: 445 us -> 529 us
  other arithmetic: 50.7 us -> 63.3 us
    all_gather x0 -> x3, waiting for transfers between devices: none -> 240 us  [body(): summed_power = jnp.sum(lax.all_gather(probe_power, 'mode'), axis=0)]
    psum x3 -> x0, waiting for transfers between devices: 154 us -> none  [body(): summed_power = lax.psum(probe_power, 'mode')]
    reduce_sum x0 -> x3, other arithmetic: none -> 11.1 us  [body(): summed_power = jnp.sum(lax.all_gather(probe_power, 'mode'), axis=0)]
where the time goes in v1:
time: 918 us; the launch traced here: 909 us
  waiting for transfers between devices  529 us (58%)
  matrix products  131 us (14%)
  local copies, waits for them, and re-layouts  102 us (11%)
  other arithmetic  63.3 us (7%)
  blocking collectives  37.5 us (4%)
  between operations  31.3 us (3%)
  starting transfers between devices  13.6 us (1%)
    psum x3, waiting for transfers between devices, body(): grad_real, grad_imag = lax.psum((grad_real, grad_imag), 'mode')  254 us
    all_gather x3, waiting for transfers between devices, body(): summed_power = jnp.sum(lax.all_gather(probe_power, 'mode'), axis=0)  240 us
    dynamic_update_slice x12, local copies, waits for them, and re-layouts, body(): lax.dynamic_update_slice(frame_grad, current + jnp.stack([grad_real[slot]...  79.7 us
    dot_general x6, matrix products, transform(): jnp.einsum('jk,bkl->bjl', stacked_rows, part_imag, precision=highest)  43.6 us
    dot_general x6, matrix products, transform(): jnp.einsum('jk,bkl->bjl', stacked_rows, part_real, precision=highest)  43.4 us
    psum x3, blocking collectives, body(): square_sum = lax.psum(jnp.sum(gradient * gradient), 'strip')  37.5 us
    ppermute x6, waiting for transfers between devices, from_behind(): return lax.ppermute(block, axis, route)  34.3 us
    dot_general x6, matrix products, transform(): jnp.einsum('bjk,kl->bjl', middle_imag, stacked_cols, precision=highest)  22.2 us
  transfers between devices with their start and end apart: 12, of which 11 were waited for; matrix products, arithmetic and copies ran while one was open for 1% of the time, Pallas kernels for 0%

profile of v1, /device:TPU:4, one launch (start us, length us, event | category | flops | bytes accessed | tf_op | source)
XLA Modules:
  0.0 908.6 jit_solution(3797961129989030444)
XLA Ops:
  31.6 7.1 convolution_bitcast_fusion.10
  38.7 7.3 convolution_bitcast_fusion.11
  58.5 80.4 %all-gather.7.cloned.1.call-done = f32[16,256,256]{2,1,0:T(8,128)} async-done(((f32[4,256,256]{2,1,0:T(8,128)}), f32[16,256,256]{2,1,0:T(8,128)}) %all-gather.7.cloned.1.call-update) | async-done | bytes 4194320 | tf_op jit(solution)/shard_map/all_gather | solution.py:84
  148.3 7.2 convolution_bitcast_fusion.9
  155.5 7.4 convolution_bitcast_fusion.8
  172.5 84.8 %all-reduce.11.cloned.1.call-done = (f32[4,256,256]{2,1,0:T(8,128)}, f32[4,256,256]{2,1,0:T(8,128)}) async-done(((f32[4,256,256]{2,1,0:T(8,128)}, f32[4,256,256]{2,1,0:T(8,128)}), (f32[4,256,256]{2,1,0:T(8,128)}, f32[4,256,256]{2,1,0:T(8,128)})) %all-reduce.11.cloned.1.call-update) | async-done | bytes 2097168 | tf_op jit(solution)/shard_map/psum | solution.py:95
  260.5 6.6 dynamic_update_slice.36
  274.9 8.1 dynamic_update_slice.38
  284.2 6.6 dynamic_update_slice.39
  292.8 8.1 collective-permute-done.1
  302.5 12.5 %psum.65 = f32[]{:T(128)} all-reduce(f32[]{:T(128)} %multiply_reduce_fusion.2), channel_id=1, replica_groups=mesh['strip'=8,'mode'=4] {'strip'}, use_global_device_ids=true, to_apply=%region_7.8 | all-reduce | flops 1 | bytes 8 | tf_op jit(solution)/shard_map/psum | solution.py:107
  326.3 7.1 convolution_bitcast_fusion.6
  333.4 7.3 convolution_bitcast_fusion.7
  352.2 80.0 %all-gather.9.cloned.1.call-done = f32[16,256,256]{2,1,0:T(8,128)} async-done(((f32[4,256,256]{2,1,0:T(8,128)}), f32[16,256,256]{2,1,0:T(8,128)}) %all-gather.9.cloned.1.call-update) | async-done | bytes 4194320 | tf_op jit(solution)/shard_map/all_gather | solution.py:84
  441.6 7.2 convolution_bitcast_fusion.5
  448.8 7.4 convolution_bitcast_fusion.4
  465.7 84.8 %all-reduce.9.cloned.1.call-done = (f32[4,256,256]{2,1,0:T(8,128)}, f32[4,256,256]{2,1,0:T(8,128)}) async-done(((f32[4,256,256]{2,1,0:T(8,128)}, f32[4,256,256]{2,1,0:T(8,128)}), (f32[4,256,256]{2,1,0:T(8,128)}, f32[4,256,256]{2,1,0:T(8,128)})) %all-reduce.9.cloned.1.call-update) | async-done | bytes 2097168 | tf_op jit(solution)/shard_map/psum | solution.py:95
  553.7 6.6 dynamic_update_slice.40
  568.1 8.1 dynamic_update_slice.42
  577.4 6.6 dynamic_update_slice.43
  586.0 8.1 collective-permute-done.3
  595.7 12.5 %psum.68 = f32[]{:T(128)} all-reduce(f32[]{:T(128)} %multiply_reduce_fusion.1), channel_id=1, replica_groups=mesh['strip'=8,'mode'=4] {'strip'}, use_global_device_ids=true, to_apply=%region_15.16 | all-reduce | flops 1 | bytes 8 | tf_op jit(solution)/shard_map/psum | solution.py:107
  619.5 7.1 convolution_bitcast_fusion.2
  626.6 7.2 convolution_bitcast_fusion.3
  645.2 80.2 %all-gather.11.cloned.1.call-done = f32[16,256,256]{2,1,0:T(8,128)} async-done(((f32[4,256,256]{2,1,0:T(8,128)}), f32[16,256,256]{2,1,0:T(8,128)}) %all-gather.11.cloned.1.call-update) | async-done | bytes 4194320 | tf_op jit(solution)/shard_map/all_gather | solution.py:84
  735.1 7.2 convolution_bitcast_fusion.1
  742.3 7.6 convolution_bitcast_fusion
  759.4 84.8 %all-reduce.7.cloned.1.call-done = (f32[4,256,256]{2,1,0:T(8,128)}, f32[4,256,256]{2,1,0:T(8,128)}) async-done(((f32[4,256,256]{2,1,0:T(8,128)}, f32[4,256,256]{2,1,0:T(8,128)}), (f32[4,256,256]{2,1,0:T(8,128)}, f32[4,256,256]{2,1,0:T(8,128)})) %all-reduce.7.cloned.1.call-update) | async-done | bytes 2097168 | tf_op jit(solution)/shard_map/psum | solution.py:95
  847.2 6.8 dynamic_update_slice.44
  861.7 8.1 dynamic_update_slice.46
  878.5 8.1 collective-permute-done.5
  887.5 12.5 %psum.71 = f32[]{:T(128)} all-reduce(f32[]{:T(128)} %multiply_reduce_fusion), channel_id=1, replica_groups=mesh['strip'=8,'mode'=4] {'strip'}, use_global_device_ids=true, to_apply=%region_23.24 | all-reduce | flops 1 | bytes 8 | tf_op jit(solution)/shard_map/psum | solution.py:107
  (136 shorter events, 176.5 us)
Async XLA Ops:
  6.5 23.4 %copy-start.11 = (f32[2,2,256,256]{3,2,1,0:T(8,128)S(1)}, f32[2,2,256,256]{3,2,1,0:T(8,128)}, u32[]{:S(2)}) copy-start(f32[2,2,256,256]{3,2,1,0:T(8,128)} %param.5) | copy-start | bytes 3145732
  6.5 132.3 %all-gather.7.cloned.1.call-start = ((), (), s32[]{:S(2)}) async-start(), calls=%async_computation | async-start | bytes 5242880 | tf_op jit(solution)/shard_map/all_gather | solution.py:84
  8.4 21.7 %collective-permute-start = (f32[2,128,384]{2,1,0:T(8,128)}, f32[2,128,384]{2,1,0:T(8,128)S(1)}, u32[]{:S(2)}, u32[]{:S(2)}) collective-permute-start(f32[2,128,384]{2,1,0:T(8,128)} %slice.359), channel_id=1, source_target_pairs={{4,0},{8,4},{12,8},{16,12},{20,16},{24,20},{28,24},{5,1},{9,5},{13... | collective-permute-start | bytes 1179656 | tf_op jit(solution)/shard_map/ppermute | solution.py:17
  49.7 3.7 copy-start
  53.4 1.9 copy-start.1
  57.5 199.9 %all-reduce.11.cloned.1.call-start = ((), (), s32[]{:S(2)}) async-start(), calls=%async_computation.5 | async-start | bytes 4194304 | tf_op jit(solution)/shard_map/psum | solution.py:95
  138.9 3.7 copy-start.7
  172.5 259.7 %all-gather.9.cloned.1.call-start = ((), (), s32[]{:S(2)}) async-start(), calls=%async_computation.1 | async-start | bytes 5242880 | tf_op jit(solution)/shard_map/all_gather | solution.py:84
  257.3 2.2 copy-start.12
  290.8 10.0 %collective-permute-start.1 = (f32[2,128,384]{2,1,0:T(8,128)S(1)}, f32[2,128,384]{2,1,0:T(8,128)S(1)}, u32[]{:S(2)}, u32[]{:S(2)}) collective-permute-start(f32[2,128,384]{2,1,0:T(8,128)S(1)} %slice.485), channel_id=1, source_target_pairs={{0,4},{4,8},{8,12},{12,16},{16,20},{20,24},{24,28},{1,5},{5,9},{9,... | collective-permute-start | bytes 1179656 | tf_op jit(solution)/shard_map/ppermute | solution.py:17
  300.9 0.7 copy-start.10
  317.0 8.6 copy-start.6
  317.0 7.2 collective-permute-start.2
  344.4 3.7 copy-start.4
  348.1 1.9 copy-start.5
  351.8 198.7 %all-reduce.9.cloned.1.call-start = ((), (), s32[]{:S(2)}) async-start(), calls=%async_computation.4 | async-start | bytes 4194304 | tf_op jit(solution)/shard_map/psum | solution.py:95
  432.2 3.7 copy-start.8
  465.7 259.7 %all-gather.11.cloned.1.call-start = ((), (), s32[]{:S(2)}) async-start(), calls=%async_computation.2 | async-start | bytes 5242880 | tf_op jit(solution)/shard_map/all_gather | solution.py:84
  550.5 2.2 copy-start.13
  584.0 10.0 %collective-permute-start.3 = (f32[2,128,384]{2,1,0:T(8,128)S(1)}, f32[2,128,384]{2,1,0:T(8,128)S(1)}, u32[]{:S(2)}, u32[]{:S(2)}) collective-permute-start(f32[2,128,384]{2,1,0:T(8,128)S(1)} %slice.515), channel_id=1, source_target_pairs={{0,4},{4,8},{8,12},{12,16},{16,20},{20,24},{24,28},{1,5},{5,9},{9,... | collective-permute-start | bytes 1179656 | tf_op jit(solution)/shard_map/ppermute | solution.py:17
  594.1 0.7 copy-start.9
  610.3 7.2 collective-permute-start.4
  637.6 3.7 copy-start.2
  641.4 1.9 copy-start.3
  645.0 199.2 %all-reduce.7.cloned.1.call-start = ((), (), s32[]{:S(2)}) async-start(), calls=%async_computation.3 | async-start | bytes 4194304 | tf_op jit(solution)/shard_map/psum | solution.py:95
  844.2 2.1 copy-start.14
  876.6 10.0 %collective-permute-start.5 = (f32[2,128,384]{2,1,0:T(8,128)S(1)}, f32[2,128,384]{2,1,0:T(8,128)S(1)}, u32[]{:S(2)}, u32[]{:S(2)}) collective-permute-start(f32[2,128,384]{2,1,0:T(8,128)S(1)} %slice.545), channel_id=1, source_target_pairs={{0,4},{4,8},{8,12},{12,16},{16,20},{20,24},{24,28},{1,5},{5,9},{9,... | collective-permute-start | bytes 1179656 | tf_op jit(solution)/shard_map/ppermute | solution.py:17
Sparse Core Ops, SparseCore 0:
  57.6 81.2 all-gather.6
  172.6 84.6 all-reduce.10
  351.9 80.2 all-gather.8
  465.8 84.6 all-reduce.8
  645.1 80.2 all-gather.10
  759.5 84.6 all-reduce.6
